TPU v7x, 128 devices: a whole 4x4x4 slice. The times are simulated.
128 devices in a mesh: row: 16 (over y_lo, x, core), col: 8 (over z, y_hi).
Axes of the slice: x: 4, y: 4 (y_hi: 2, y_lo: 2; y = y_hi * 2 + y_lo), z: 4, core: 2. Of those that a mesh axis runs over, the one named last changes fastest.
Arguments:
- grad_out: bfloat16 [2048, 16384], P('col', 'row'), may hold values from -6 to 6
- gate_act: bfloat16 [2048, 26624], P('row', 'col'), may hold values from -8 to 8
- up_act: bfloat16 [2048, 26624], P('row', 'col'), may hold values from -6 to 6
- down_weight: bfloat16 [26624, 16384], P('col', 'row'), may hold values from -0.046875 to 0.046875
Outputs:
- grad_gate: bfloat16 [2048, 26624], P('row', 'col')
- grad_up: bfloat16 [2048, 26624], P('row', 'col')
- grad_down: bfloat16 [26624, 16384], P('col', 'row')
All inputs are finite; a program needn't handle non-finite values.
Results may differ from a plain program's by a relative error of at most 0.0049.
Values may be sent and summed in bfloat16 or wider, within the bound.
A program may use at most 448 MiB of HBM per device.

v0:
```python
import jax
import jax.numpy as jnp
from jax import lax
from jax.sharding import PartitionSpec as P


def swiglu_grads(grad_hidden, gate_act, up_act):
    gate_val = gate_act.astype(jnp.float32)
    up_val = up_act.astype(jnp.float32)
    sigmoid_g = jax.nn.sigmoid(gate_val)
    act_val = gate_val * sigmoid_g
    hidden = (act_val * up_val).astype(jnp.bfloat16)
    grad_gate = (grad_hidden * up_val * sigmoid_g * (1.0 + gate_val * (1.0 - sigmoid_g))).astype(
        jnp.bfloat16
    )
    grad_up = (grad_hidden * act_val).astype(jnp.bfloat16)
    return (hidden, grad_gate, grad_up)


def local(grad_out, gate_act, up_act, down_weight):
    dy_cols = lax.all_gather(grad_out, "col", axis=0, tiled=True)
    dy_rows = dy_cols
    grad_hidden = lax.psum_scatter(
        lax.dot_general(
            dy_rows, down_weight, (((1,), (1,)), ((), ())), preferred_element_type=jnp.float32
        ),
        "row",
        scatter_dimension=0,
        tiled=True,
    )
    hidden, grad_gate, grad_up = swiglu_grads(grad_hidden, gate_act, up_act)
    dy_rows = dy_cols
    grad_down = lax.dot_general(
        lax.all_gather(hidden, "row", axis=0, tiled=True),
        dy_rows,
        (((0,), (0,)), ((), ())),
        preferred_element_type=jnp.float32,
    ).astype(jnp.bfloat16)
    return (grad_gate, grad_up, grad_down)


def solution(mesh):
    return jax.shard_map(
        local,
        mesh=mesh,
        in_specs=(P("col", "row"), P("row", "col"), P("row", "col"), P("col", "row")),
        out_specs=(P("row", "col"), P("row", "col"), P("col", "row")),
        check_vma=False,
    )
```

profile of v0, /device:TPU:1, one launch (start us, length us, event | category | flops | bytes accessed | tf_op | source)
XLA Modules:
  0.0 362.6 jit_solution(8168998493723738777)
XLA Ops:
  7.2 0.0 all-gather.3.cloned.1.call-start
  7.2 0.7 all-gather.3.cloned.1.call-update
  7.9 0.0 reduce-scatter.2.cloned.1.call-start
  7.9 76.2 %all-gather.3.cloned.1.call-done = bf16[2048,1024]{1,0:T(8,128)(2,1)} async-done(((bf16[256,1024]{1,0:T(8,128)(2,1)}), bf16[2048,1024]{1,0:T(8,128)(2,1)}) %all-gather.3.cloned.1.call-update) | async-done | bytes 4194320 | tf_op jit(solution)/shard_map/all_gather | solution.py:21
  84.1 21.7 %fusion.8 = f32[2048,3328]{1,0:T(8,128)} fusion(bf16[2048,1024]{1,0:T(8,128)(2,1)} %all-gather.3.cloned.1.call-done, bf16[3328,1024]{1,0:T(8,128)(2,1)} %param.7), kind=kOutput, calls=%fused_computation.15 | convolution fusion | flops 13958643712 | bytes 38273024 | tf_op jit(solution)/shard_map/dot_general | solution.py:24
  105.8 0.0 copy-start
  105.8 0.0 copy-start.1
  105.8 0.0 reduce-scatter.2.cloned.1.call-update
  105.9 0.2 all-gather.5.cloned.1.call-start
  106.1 148.2 %reduce-scatter.2.cloned.1.call-done = f32[128,3328]{1,0:T(8,128)} async-done(((f32[2048,3328]{1,0:T(8,128)}), f32[128,3328]{1,0:T(8,128)}) %reduce-scatter.2.cloned.1.call-update) | async-done | bytes 1703952 | tf_op jit(solution)/shard_map/reduce_scatter | solution.py:23
  254.3 0.0 copy-done
  254.3 0.0 copy-done.1
  254.3 3.7 %multiply_convert_fusion = (bf16[128,3328]{1,0:T(8,128)(2,1)}, bf16[128,3328]{1,0:T(8,128)(2,1)}, bf16[128,3328]{1,0:T(8,128)(2,1)}) fusion(f32[128,3328]{1,0:T(8,128)} %reduce-scatter.2.cloned.1.call-done, bf16[128,3328]{1,0:T(8,128)(2,1)S(1)} %copy-done, bf16[128,3328]{1,0:T(8,128)(2,1)S(1)} %copy-done.1), kind=kLoop, calls=%fused_computation.14 | loop fusion | flops 7241728 | bytes 5963776 | tf_op jit(solution)/shard_map/convert_element_type | solution.py:16
  258.0 0.0 all-gather.5.cloned.1.call-update
  258.0 77.5 %all-gather.5.cloned.1.call-done = bf16[2048,3328]{1,0:T(8,128)(2,1)} async-done(((bf16[128,3328]{1,0:T(8,128)(2,1)}), bf16[2048,3328]{1,0:T(8,128)(2,1)}) %all-gather.5.cloned.1.call-update) | async-done | bytes 13631504 | tf_op jit(solution)/shard_map/all_gather | solution.py:34
  335.5 20.6 %convolution_convert_fusion = bf16[3328,1024]{1,0:T(8,128)(2,1)} fusion(bf16[2048,3328]{1,0:T(8,128)(2,1)} %all-gather.5.cloned.1.call-done, bf16[2048,1024]{1,0:T(8,128)(2,1)} %all-gather.3.cloned.1.call-done), kind=kOutput, calls=%fused_computation | convolution fusion | flops 13962051584 | bytes 24641536 | tf_op jit(solution)/shard_map/dot_general | solution.py:33
Async XLA Ops:
  7.2 76.9 %all-gather.3.cloned.1.call-start = ((), (), s32[]{:S(2)}) async-start(), calls=%async_computation.1 | async-start | bytes 4718592 | tf_op jit(solution)/shard_map/all_gather | solution.py:21
  7.9 246.4 %reduce-scatter.2.cloned.1.call-start = ((), (), s32[]{:S(2)}) async-start(), calls=%async_computation.2 | async-start | bytes 28966912 | tf_op jit(solution)/shard_map/reduce_scatter | solution.py:23
  105.8 148.5 %copy-start = (bf16[128,3328]{1,0:T(8,128)(2,1)S(1)}, bf16[128,3328]{1,0:T(8,128)(2,1)}, u32[]{:S(2)}) copy-start(bf16[128,3328]{1,0:T(8,128)(2,1)} %param.5) | copy-start | bytes 2555908
  105.8 148.5 %copy-start.1 = (bf16[128,3328]{1,0:T(8,128)(2,1)S(1)}, bf16[128,3328]{1,0:T(8,128)(2,1)}, u32[]{:S(2)}) copy-start(bf16[128,3328]{1,0:T(8,128)(2,1)} %param.6) | copy-start | bytes 2555908
  105.9 229.6 %all-gather.5.cloned.1.call-start = ((), (), s32[]{:S(2)}) async-start(), calls=%async_computation.3 | async-start | bytes 14483456 | tf_op jit(solution)/shard_map/all_gather | solution.py:34
Sparse Core Ops, SparseCore 0:
  10.3 73.7 all-gather.2
  106.0 148.2 reduce-scatter.1
  258.2 77.2 all-gather.4
where the time goes:
time: 363 us
  waiting for transfers between devices  303 us (83%)
  matrix products  42.3 us (12%)
  between operations  13.7 us (4%)
  other arithmetic  3.7 us (1%)
    reduce_scatter x1, waiting for transfers between devices, local(): lax.psum_scatter(lax.dot_general(dy_rows, down_weight, (((1,), (1,)), (()...  148 us
    all_gather x1, waiting for transfers between devices, local(): lax.all_gather(hidden, 'row', axis=0, tiled=True)  77.5 us
    all_gather x1, waiting for transfers between devices, local(): dy_cols = lax.all_gather(grad_out, 'col', axis=0, tiled=True)  76.2 us
    dot_general x1, matrix products, local(): lax.dot_general(dy_rows, down_weight, (((1,), (1,)), ((), ())), preferred...  21.7 us
    dot_general x1, matrix products, local(): lax.dot_general(lax.all_gather(hidden, 'row', axis=0, tiled=True), dy_row...  20.6 us
  transfers between devices with their start and end apart: 3, of which 3 were waited for; matrix products, arithmetic and copies ran while one was open for 0% of the time, Pallas kernels for 0%

commit v1 on v0

v1 whole, which is shorter than its diff:
```python
import functools

import jax
import jax.numpy as jnp
from jax import lax
from jax.experimental import pallas as pl
from jax.experimental.pallas import tpu as pltpu
from jax.sharding import PartitionSpec as P

MESH = pl.DeviceIdType.MESH
BF = jnp.bfloat16
F32 = jnp.float32
NT = (((1,), (1,)), ((), ()))
NN = (((1,), (0,)), ((), ()))

TB = 256
DB = 1024
FH = 1664
RA = 1024
RB = FH - RA
HB = RB // 2
A = pl.ds(0, RA)
B = pl.ds(RA, RB)
B0 = pl.ds(RA, HB)
B1 = pl.ds(RA + HB, HB)
MT = 832
NTILE = 256


def at(i, size):
    return pl.ds(pl.multiple_of(i * size, size), size)


def kernel(dy_ref, gate_ref, up_ref, w_ref, gg_ref, gu_ref, gd_ref,
           wv, dyv, ht, g, u, part, r1p, r1m, r2pc, r2ps, r2mc, r2ms, ry, by, b1p, b1m, b2p, b2m,
           gdv, og, ou, ss, rs, ls):
    row, col = lax.axis_index("row"), lax.axis_index("col")
    yl, x, q = row // 8, (row // 2) % 4, row % 2
    z, yh = col // 2, col % 2
    o = 1 - q

    def dev(yl, x, q, z, yh):
        return {"row": (yl * 4 + x) * 2 + q, "col": z * 2 + yh}

    core = dev(yl, x, o, z, yh)
    xp = dev(yl, (x + 1) % 4, q, z, yh)
    xm = dev(yl, (x + 3) % 4, q, z, yh)
    ylp = dev(1 - yl, x, q, z, yh)
    zp = dev(yl, x, q, (z + 1) % 4, yh)
    zm = dev(yl, x, q, (z + 3) % 4, yh)
    yhp = dev(yl, x, q, z, 1 - yh)

    ids = {}

    def remote(name, src, dst, to):
        i = ids.setdefault(name, len(ids))
        return pltpu.make_async_remote_copy(src, dst, ss.at[i], rs.at[i], device_id=to, device_id_type=MESH)

    def cb(dz, fl):
        return ((z + dz) % 4) * 2 + (yh + fl) % 2

    def dyb(p, dz, fl):
        return dyv.at[p, at(cb(dz, fl), TB), :]

    def kb(fl, dx):
        return ((yl + fl) % 2) * 4 + (x + dx) % 4

    def htb(rows, fl, dx):
        return ht.at[rows, at(kb(fl, dx), TB)]

    def pt(fl, dx, rows):
        return part.at[kb(fl, dx), rows, :]

    def same(name, ref, to):
        return remote(name, ref, ref, to)

    half_q, half_o = at(q, FH), at(o, FH)
    tok_q, tok_o = at(q, 128), at(o, 128)

    D = {
        "G": remote("G", gate_ref.at[:, half_o], g.at[tok_q, :], core),
        "U": remote("U", up_ref.at[:, half_o], u.at[tok_q, :], core),
        "D1": remote("D1", dy_ref, dyb(q, 0, 0), core),
        "D2": remote("D2", dy_ref, dyb(q, 0, 0), yhp),
        "D3": remote("D3", dy_ref, dyb(q, 0, 0), zp),
        "D4": remote("D4", dy_ref, dyb(q, 0, 0), zm),
        "W": remote("W", w_ref.at[half_o, :], wv.at[q], core),
        "D5": same("D5", dyb(q, 3, 0), zp),
        "D6": same("D6", dyb(q, 0, 1), zp),
        "D7": same("D7", dyb(q, 0, 1), zm),
        "D8": same("D8", dyb(q, 1, 1), zm),
        "HA1": same("HA1", htb(A, 0, 0), xp),
        "HA2": same("HA2", htb(A, 0, 0), xm),
        "HB1": same("HB1", htb(B, 0, 0), xp),
        "HB2": same("HB2", htb(B, 0, 0), xm),
        "HYA": same("HYA", htb(A, 0, 0), ylp),
        "HYB": same("HYB", htb(B, 0, 0), ylp),
        "HB3": same("HB3", htb(B0, 0, 3), xp),
        "HB4": same("HB4", htb(B1, 0, 1), xm),
        "HYB2": same("HYB2", htb(B, 0, 3), ylp),
        "HYB3": same("HYB3", htb(B, 0, 1), ylp),
        "HYB4": same("HYB4", htb(B0, 0, 2), ylp),
        "HYB5": same("HYB5", htb(B1, 0, 2), ylp),
        "HA3": same("HA3", htb(A, 1, 0), xp),
        "HA4": same("HA4", htb(A, 1, 0), xm),
        "HA5": same("HA5", htb(A, 0, 3), xp),
        "HA6": same("HA6", htb(A, 1, 1), xm),
        "S1P": remote("S1P", pt(0, 2, A), r1p, xp),
        "S1M": remote("S1M", pt(1, 2, A), r1m, xm),
        "S2PS": remote("S2PS", pt(1, 1, A), r2ps, xp),
        "S2MS": remote("S2MS", pt(0, 3, A), r2ms, xm),
        "S2PC": remote("S2PC", pt(0, 1, A), r2pc, xp),
        "S2MC": remote("S2MC", pt(1, 3, A), r2mc, xm),
        "SYA": remote("SYA", pt(1, 0, A), ry, ylp),
        "SB1P": remote("SB1P", pt(0, 2, B0), b1p, xp),
        "SB1M": remote("SB1M", pt(0, 2, B1), b1m, xm),
        "SB2P": remote("SB2P", pt(0, 1, B), b2p, xp),
        "SB2M": remote("SB2M", pt(0, 3, B), b2m, xm),
    }
    for dx in range(4):
        D[f"SYB{dx}"] = remote(f"SYB{dx}", pt(1, dx, B), by.at[(x + dx) % 4], ylp)
    for dz, fl in ((3, 0), (1, 0), (0, 1), (2, 0), (1, 1), (3, 1), (2, 1)):
        D[f"C{dz}{fl}"] = same(f"C{dz}{fl}", dyb(q, dz, fl), core)
    for m in range(2):
        D[f"GD{m}"] = remote(f"GD{m}", gdv.at[o, pl.ds(m * MT, MT), :],
                             gd_ref.at[pl.ds(pl.multiple_of(q * FH + m * MT, MT), MT), :], core)
    for name, start, size in (("A", 0, RA), ("B", RA, RB)):
        there = pl.ds(pl.multiple_of(q * FH + start, 128), size)
        here = pl.ds(start, size)
        D["OG" + name] = remote("OG" + name, og.at[tok_o, here], gg_ref.at[:, there], core)
        D["OU" + name] = remote("OU" + name, ou.at[tok_o, here], gu_ref.at[:, there], core)

    def go(*names):
        for n in names:
            D[n].start()

    def got(*names):
        for n in names:
            D[n].wait_recv()

    local = {
        "g": pltpu.make_async_copy(gate_ref.at[:, half_q], g.at[tok_q, :], ls.at[0]),
        "u": pltpu.make_async_copy(up_ref.at[:, half_q], u.at[tok_q, :], ls.at[1]),
        "dy": pltpu.make_async_copy(dy_ref, dyb(q, 0, 0), ls.at[2]),
        "w": pltpu.make_async_copy(w_ref.at[half_q, :], wv.at[q], ls.at[3]),
    }
    for n in ("g", "u", "dy", "w"):
        local[n].start()

    bar = pltpu.get_barrier_semaphore()
    for to in (core, xp, xm, ylp, zp, zm, yhp):
        pl.semaphore_signal(bar, inc=1, device_id=to, device_id_type=MESH)
    pl.semaphore_wait(bar, 7)

    go("G", "U", "D2", "D3", "D4", "D1", "W")

    local["g"].wait()
    local["u"].wait()
    got("G", "U")

    def hidden(i, _):
        s = at(i, 128)
        gv, uv = g[:, s].astype(F32), u[:, s].astype(F32)
        h = gv * jax.nn.sigmoid(gv) * uv
        ht[s, at(kb(0, 0), TB)] = h.T.astype(BF)
        return 0

    lax.fori_loop(0, FH // 128, hidden, 0)
    go("HYA", "HB1", "HB2", "HA1", "HA2", "HYB")

    order = ((0, 0), (3, 0), (1, 0), (0, 1), (2, 0), (1, 1), (3, 1), (2, 1))

    def serve1(s):
        if s == 0:
            local["dy"].wait()
            local["w"].wait()
            got("W", "D1")
        elif s == 1:
            got("D3")
            go("D5", "C30")
            got("D4")
            go("C10")
            got("D2")
            go("D7", "D6", "C01")
            got("C30")
        elif s == 2:
            got("HB1", "HB2")
            go("HB3", "HB4", "HYB2", "HYB3")
            got("C10")
        elif s == 3:
            got("HA1", "HA2", "HYA")
            go("HA5", "HA4", "HA3")
            got("C01")
        elif s == 4:
            got("D5")
            go("C20")
            got("D7")
            go("D8", "C11")
            got("HB3", "HB4")
            go("HYB4", "HYB5")
            got("C20")
        elif s == 5:
            got("C11")
        elif s == 6:
            got("D6")
            go("C31")
            got("HA4")
            go("HA6")
            got("D8")
            go("C21")
            got("C31")
        elif s == 7:
            got("C21")

    def step1(s, _):
        for i in range(8):
            pl.when(s == i)(functools.partial(serve1, i))
        dz = fl = jnp.int32(0)
        for i, (a, b) in enumerate(order):
            dz = jnp.where(s == i, a, dz)
            fl = jnp.where(s == i, b, fl)
        c = cb(dz, fl)

        def tile(m, _):
            rows = at(m, MT)
            acc = None
            for p in range(2):
                d = lax.dot_general(wv[p, rows, :], dyv[p, at(c, TB), :], NT, preferred_element_type=F32)
                acc = d if acc is None else acc + d
            part[c, rows, :] = acc.astype(BF)
            return 0

        lax.fori_loop(0, FH // MT, tile, 0)
        return 0

    lax.fori_loop(0, 8, step1, 0)

    go("S1P", "S1M", "S2PS", "S2MS", "SYB2", "SYB1", "SYB3", "SYB0")

    def add(k, start, size, *others):
        def chunk(i, _):
            t = part[k, pl.ds(pl.multiple_of(start + i * 64, 64), 64), :].astype(F32)
            for ref, off in others:
                t = t + ref[pl.ds(pl.multiple_of(off + i * 64, 64), 64), :].astype(F32)
            part[k, pl.ds(pl.multiple_of(start + i * 64, 64), 64), :] = t.astype(BF)
            return 0

        lax.fori_loop(0, size // 64, chunk, 0)

    def serve2(s):
        if s == 0:
            got("HYB", "HYB2", "HYB3", "HYB4", "HYB5", "HA3", "HA5", "HA6")
        elif s == 8:
            got("S1P", "S1M")
            add(kb(0, 1), 0, RA, (r1p, 0))
            go("S2PC")
            add(kb(1, 3), 0, RA, (r1m, 0))
            go("S2MC")
            got("SYB2")
            add(kb(0, 2), RA, RB, (by.at[(x + 2) % 4], 0))
            go("SB1P", "SB1M", "GD0", "GD1")

    def step2(s, _):
        for i in (0, 8):
            pl.when(s == i)(functools.partial(serve2, i))
        p = jnp.where(s < 8, o, q)
        m = (s // 4) % 2
        n = s % 4
        rows, cols = at(m, MT), at(n, NTILE)
        d = lax.dot_general(ht[rows, :], dyv[p, :, cols], NN, preferred_element_type=F32)
        gdv[p, rows, cols] = d.astype(BF)
        return 0

    lax.fori_loop(0, 16, step2, 0)

    gd_out = pltpu.make_async_copy(gdv.at[q], gd_ref.at[half_q, :], ls.at[0])
    gd_out.start()

    got("SYB1", "SYB3", "SYB0")
    add(kb(0, 1), RA, RB, (by.at[(x + 1) % 4], 0))
    add(kb(0, 3), RA, RB, (by.at[(x + 3) % 4], 0))
    got("SB1P")
    add(kb(0, 1), RA, HB, (b1p, 0))
    go("SB2P")
    got("SB1M")
    add(kb(0, 3), RA + HB, HB, (b1m, 0))
    go("SB2M")

    got("S2PS", "S2MC", "S2PC", "S2MS")
    add(kb(1, 0), 0, RA, (r2ps, 0), (r2mc, 0))
    go("SYA")

    def final(first, last, *others):
        def tile(i, _):
            s = at(i, 128)
            t = part[kb(0, 0), s, :].astype(F32)
            for ref in others:
                t = t + ref[at(i - first, 128), :].astype(F32)
            gh = t.T
            gv, uv = g[:, s].astype(F32), u[:, s].astype(F32)
            sig = jax.nn.sigmoid(gv)
            og[:, s] = (gh * uv * sig * (1.0 + gv * (1.0 - sig))).astype(BF)
            ou[:, s] = (gh * (gv * sig)).astype(BF)
            return 0

        lax.fori_loop(first, last, tile, 0)

    outs = [gd_out]

    def emit(name, start, size, i):
        go("OG" + name, "OU" + name)
        there = pl.ds(pl.multiple_of(q * FH + start, 128), size)
        for ref, dst in ((og, gg_ref), (ou, gu_ref)):
            c = pltpu.make_async_copy(ref.at[tok_q, pl.ds(start, size)], dst.at[:, there], ls.at[i])
            c.start()
            outs.append(c)
            i += 1

    got("SB2P", "SB2M")
    final(RA // 128, FH // 128, by.at[x], b2p, b2m)
    emit("B", RA, RB, 1)
    got("SYA")
    final(0, RA // 128, r2pc, r2ms, ry)
    emit("A", 0, RA, 3)

    for c in outs:
        c.wait()
    got("GD0", "GD1", "OGA", "OUA", "OGB", "OUB")
    for n in D:
        D[n].wait_send()


def local(grad_out, gate_act, up_act, down_weight):
    hbm = pl.BlockSpec(memory_space=pl.ANY)
    block = lambda *s: pltpu.VMEM(s, BF)
    return pl.pallas_call(
        kernel,
        out_shape=(
            jax.ShapeDtypeStruct(gate_act.shape, BF),
            jax.ShapeDtypeStruct(up_act.shape, BF),
            jax.ShapeDtypeStruct(down_weight.shape, BF),
        ),
        in_specs=[hbm] * 4,
        out_specs=(hbm,) * 3,
        scratch_shapes=[
            block(2, FH, DB), block(2, 8 * TB, DB), block(FH, 8 * TB), block(TB, FH), block(TB, FH),
            block(8, FH, TB),
            block(RA, TB), block(RA, TB), block(RA, TB), block(RA, TB), block(RA, TB), block(RA, TB), block(RA, TB),
            block(4, RB, TB), block(HB, TB), block(HB, TB), block(RB, TB), block(RB, TB),
            block(2, FH, DB), block(TB, FH), block(TB, FH),
            pltpu.SemaphoreType.DMA((60,)), pltpu.SemaphoreType.DMA((60,)), pltpu.SemaphoreType.DMA((8,)),
        ],
        compiler_params=pltpu.CompilerParams(
            collective_id=0, has_side_effects=True, vmem_limit_bytes=60 * 2**20
        ),
        name="swiglu_down_backward",
    )(grad_out, gate_act, up_act, down_weight)


def solution(mesh):
    return jax.shard_map(
        local,
        mesh=mesh,
        in_specs=(P("col", "row"), P("row", "col"), P("row", "col"), P("col", "row")),
        out_specs=(P("row", "col"), P("row", "col"), P("col", "row")),
        check_vma=False,
    )
```

time: 363 us -> 125 us (0.34)
  waiting for transfers between devices: 303 us -> 0 us
  Pallas kernels: 0 us -> 113 us
  matrix products: 42.3 us -> 0 us
  between operations: 13.7 us -> 0.64 us
  local copies, waits for them, and re-layouts: 0.01 us -> 10.8 us
  other arithmetic: 3.7 us -> 0 us
    all_gather x2 -> x0, waiting for transfers between devices: 154 us -> none  [the longest x1 77.5 us: local(): lax.all_gather(hidden, 'row', axis=0, tiled=True)]
    reduce_scatter x1 -> x0, waiting for transfers between devices: 148 us -> none  [local(): lax.psum_scatter(lax.dot_general(dy_rows, down_weight, (((1,), (1,)), (()...]
    pallas_call x0 -> x1, Pallas kernels: none -> 113 us  [local(): pl.pallas_call(kernel, out_shape=(jax.ShapeDtypeStruct(gate_act.shape, BF...]
    dot_general x2 -> x0, matrix products: 42.3 us -> none  [the longest x1 21.7 us: local(): lax.dot_general(dy_rows, down_weight, (((1,), (1,)), ((), ())), preferred...]
    unnamed x4 -> x3, local copies, waits for them, and re-layouts: 0.01 us -> 10.8 us
    convert_element_type x1 -> x0, other arithmetic: 3.7 us -> none  [swiglu_grads(): grad_up = (grad_hidden * act_val).astype(jnp.bfloat16)]
  transfers between devices with their start and end apart: 3 -> 0, of which waited for: 3 -> 0; matrix products, arithmetic and copies ran while one was open for 0% -> 0% of each run, Pallas kernels for 0% -> 0%
where the time goes in v1:
time: 125 us
  Pallas kernels  113 us (90%)
  local copies, waits for them, and re-layouts  10.8 us (9%)
    pallas_call x1, Pallas kernels, local(): pl.pallas_call(kernel, out_shape=(jax.ShapeDtypeStruct(gate_act.shape, BF...  113 us
    unnamed x3, local copies, waits for them, and re-layouts  10.8 us

profile of v1, /device:TPU:1, one launch (start us, length us, event | category | flops | bytes accessed | tf_op | source)
XLA Modules:
  0.0 124.7 jit_solution(13185409411323889621)
XLA Ops:
  0.6 113.3 %swiglu_down_backward.1 = (bf16[128,3328]{1,0:T(8,128)(2,1)}, bf16[128,3328]{1,0:T(8,128)(2,1)}, bf16[3328,1024]{1,0:T(8,128)(2,1)}) custom-call(bf16[256,1024]{1,0:T(8,128)(2,1)} %dy_ref.1, bf16[128,3328]{1,0:T(8,128)(2,1)} %gate_ref.1, bf16[128,3328]{1,0:T(8,128)(2,1)} %up_ref.1, bf16[3328,1024]{1,0:T(8,128)(2,1)} %w_ref.1), custom_call_target="tpu_custom_call" | custom-call | tf_op jit(solution)/shard_map/swiglu_down_backward/pallas_call | solution.py:336
  113.9 2.1 %copy.10 = bf16[128,3328]{1,0:T(8,128)(2,1)} copy(bf16[128,3328]{1,0:T(8,128)(2,1)} %get-tuple-element.6) | data formatting | bytes 1703936
  116.0 2.1 %copy.11 = bf16[128,3328]{1,0:T(8,128)(2,1)} copy(bf16[128,3328]{1,0:T(8,128)(2,1)} %get-tuple-element.7) | data formatting | bytes 1703936
  118.1 6.6 %copy.12 = bf16[3328,1024]{1,0:T(8,128)(2,1)} copy(bf16[3328,1024]{1,0:T(8,128)(2,1)} %get-tuple-element.8) | data formatting | bytes 13631488

commit v2 on v1

v2 whole, which is shorter than its diff:
```python
import functools

import jax
import jax.numpy as jnp
from jax import lax
from jax.experimental import pallas as pl
from jax.experimental.pallas import tpu as pltpu
from jax.sharding import PartitionSpec as P

MESH = pl.DeviceIdType.MESH
BF = jnp.bfloat16
F32 = jnp.float32
NT = (((1,), (1,)), ((), ()))
NN = (((1,), (0,)), ((), ()))

TB = 256
DB = 1024
FH = 1664
RA = 1024
RB = FH - RA
HA = RA // 2
HB = RB // 2
HT = TB // 2
A = pl.ds(0, RA)
A0 = pl.ds(0, HA)
A1 = pl.ds(HA, HA)
B = pl.ds(RA, RB)
B0 = pl.ds(RA, HB)
B1 = pl.ds(RA + HB, HB)
MT = 832
NTILE = 256


def at(i, size):
    return pl.ds(pl.multiple_of(i * size, size), size)


def kernel(dy_ref, gate_ref, up_ref, w_ref, gg_ref, gu_ref, gd_ref,
           wv, dyv, ht, hs, gv, uv, gp, upv, part, r1p, r1m, r2pc, r2ps, r2mc, r2ms, ry, by, b1p, b1m, b2p, b2m,
           gdv, og, ou, ss, rs, ls):
    row, col = lax.axis_index("row"), lax.axis_index("col")
    yl, x, q = row // 8, (row // 2) % 4, row % 2
    z, yh = col // 2, col % 2
    o = 1 - q

    def dev(yl, x, q, z, yh):
        return {"row": (yl * 4 + x) * 2 + q, "col": z * 2 + yh}

    core = dev(yl, x, o, z, yh)
    xp = dev(yl, (x + 1) % 4, q, z, yh)
    xm = dev(yl, (x + 3) % 4, q, z, yh)
    ylp = dev(1 - yl, x, q, z, yh)
    zp = dev(yl, x, q, (z + 1) % 4, yh)
    zm = dev(yl, x, q, (z + 3) % 4, yh)
    yhp = dev(yl, x, q, z, 1 - yh)

    ids = {}

    def remote(name, src, dst, to):
        i = ids.setdefault(name, len(ids))
        return pltpu.make_async_remote_copy(src, dst, ss.at[i], rs.at[i], device_id=to, device_id_type=MESH)

    def cb(dz, fl):
        return ((z + dz) % 4) * 2 + (yh + fl) % 2

    def dyb(p, dz, fl):
        return dyv.at[p, at(cb(dz, fl), TB), :]

    def dyh(dz, fl, half):
        return dyv.at[q, at(cb(dz, fl) * 2 + half, HT), :]

    def kb(fl, dx):
        return ((yl + fl) % 2) * 4 + (x + dx) % 4

    def htb(rows, fl, dx):
        return ht.at[rows, at(kb(fl, dx), TB)]

    def hth(rows, core_of):
        return ht.at[rows, at(kb(0, 0) * 2 + core_of, HT)]

    def pt(fl, dx, rows):
        return part.at[kb(fl, dx), rows, :]

    def same(name, ref, to):
        return remote(name, ref, ref, to)

    half_q, half_o = at(q, FH), at(o, FH)

    D = {
        "HS": remote("HS", hs, hth(pl.ds(0, FH), q), core),
        "G": remote("G", gate_ref.at[:, half_o], gp, core),
        "U": remote("U", up_ref.at[:, half_o], upv, core),
        "D1": remote("D1", dy_ref, dyb(q, 0, 0), core),
        "D2": remote("D2", dy_ref, dyb(q, 0, 0), yhp),
        "D3": remote("D3", dy_ref, dyb(q, 0, 0), zp),
        "D4": remote("D4", dy_ref, dyb(q, 0, 0), zm),
        "W": remote("W", w_ref.at[half_o, :], wv.at[q], core),
        "D5a": same("D5a", dyh(3, 0, 0), zp),
        "D5b": same("D5b", dyh(1, 0, 1), zm),
        "D6": same("D6", dyb(q, 0, 1), zp),
        "D7": same("D7", dyb(q, 0, 1), zm),
        "D8a": same("D8a", dyh(3, 1, 0), zp),
        "D8b": same("D8b", dyh(1, 1, 1), zm),
        "HB1a": same("HB1a", hth(B, q), xp),
        "HB1b": same("HB1b", hth(B, o), xp),
        "HB2a": same("HB2a", hth(B, q), xm),
        "HB2b": same("HB2b", hth(B, o), xm),
        "HA1": same("HA1", htb(A, 0, 0), xp),
        "HA2": same("HA2", htb(A, 0, 0), xm),
        "HYA": same("HYA", htb(A, 0, 0), ylp),
        "HYB": same("HYB", htb(B, 0, 0), ylp),
        "HB3": same("HB3", htb(B0, 0, 3), xp),
        "HB4": same("HB4", htb(B1, 0, 1), xm),
        "HYB2": same("HYB2", htb(B, 0, 3), ylp),
        "HYB3": same("HYB3", htb(B, 0, 1), ylp),
        "HYB4": same("HYB4", htb(B0, 0, 2), ylp),
        "HYB5": same("HYB5", htb(B1, 0, 2), ylp),
        "HA3a": same("HA3a", htb(A0, 1, 0), xp),
        "HA3b": same("HA3b", htb(A1, 1, 0), xp),
        "HA4a": same("HA4a", htb(A0, 1, 0), xm),
        "HA4b": same("HA4b", htb(A1, 1, 0), xm),
        "HA5a": same("HA5a", htb(A0, 0, 3), xp),
        "HA5b": same("HA5b", htb(A1, 0, 1), xm),
        "HA6a": same("HA6a", htb(A0, 1, 3), xp),
        "HA6b": same("HA6b", htb(A1, 1, 1), xm),
        "S1P": remote("S1P", pt(0, 2, A), r1p, xp),
        "S1M": remote("S1M", pt(1, 2, A), r1m, xm),
        "SB1P": remote("SB1P", pt(0, 2, B0), b1p, xp),
        "SB1M": remote("SB1M", pt(0, 2, B1), b1m, xm),
        "SB2Pi": remote("SB2Pi", pt(0, 1, B1), b2p.at[pl.ds(HB, HB), :], xp),
        "SB2Pd": remote("SB2Pd", pt(0, 1, B0), b2p.at[pl.ds(0, HB), :], xp),
        "SB2Mi": remote("SB2Mi", pt(0, 3, B0), b2m.at[pl.ds(0, HB), :], xm),
        "SB2Md": remote("SB2Md", pt(0, 3, B1), b2m.at[pl.ds(HB, HB), :], xm),
    }
    for i, r in enumerate((A0, A1)):
        D[f"S2PS{i}"] = remote(f"S2PS{i}", pt(1, 1, r), r2ps.at[r, :], xp)
        D[f"S2MS{i}"] = remote(f"S2MS{i}", pt(0, 3, r), r2ms.at[r, :], xm)
        D[f"S2PC{i}"] = remote(f"S2PC{i}", pt(0, 1, r), r2pc.at[r, :], xp)
        D[f"S2MC{i}"] = remote(f"S2MC{i}", pt(1, 3, r), r2mc.at[r, :], xm)
        D[f"SYA{i}"] = remote(f"SYA{i}", pt(1, 0, r), ry.at[r, :], ylp)
    for dx in range(4):
        D[f"SYB{dx}"] = remote(f"SYB{dx}", pt(1, dx, B), by.at[(x + dx) % 4], ylp)
    for dz, fl in ((3, 0), (1, 0), (0, 1), (2, 0), (1, 1), (3, 1), (2, 1)):
        D[f"C{dz}{fl}"] = same(f"C{dz}{fl}", dyb(q, dz, fl), core)
    for m in range(2):
        D[f"GD{m}"] = remote(f"GD{m}", gdv.at[pl.ds(m * MT, MT), :],
                             gd_ref.at[pl.ds(pl.multiple_of(q * FH + m * MT, MT), MT), :], core)
    for name, start, size in (("0", 0, HA), ("1", HA, HA), ("2", RA, RB)):
        there = pl.ds(pl.multiple_of(q * FH + start, 128), size)
        here = pl.ds(start, size)
        D["OG" + name] = remote("OG" + name, og.at[:, here], gg_ref.at[:, there], core)
        D["OU" + name] = remote("OU" + name, ou.at[:, here], gu_ref.at[:, there], core)

    def go(*names):
        for n in names:
            D[n].start()

    def got(*names):
        for n in names:
            D[n].wait_recv()

    local = {
        "g": pltpu.make_async_copy(gate_ref, gv, ls.at[0]),
        "u": pltpu.make_async_copy(up_ref, uv, ls.at[1]),
        "dy": pltpu.make_async_copy(dy_ref, dyb(q, 0, 0), ls.at[2]),
        "w": pltpu.make_async_copy(w_ref.at[half_q, :], wv.at[q], ls.at[3]),
    }

    bar = pltpu.get_barrier_semaphore()
    for to in (core, xp, xm, ylp, zp, zm, yhp):
        pl.semaphore_signal(bar, inc=1, device_id=to, device_id_type=MESH)
    for n in ("g", "u", "dy", "w"):
        local[n].start()

    def hidden(first, last, half, dst, lanes):
        def tile(i, _):
            s = at(i, 128)
            f = pl.ds(pl.multiple_of(half * FH + i * 128, 128), 128)
            gt, ut = gv[:, f].astype(F32), uv[:, f].astype(F32)
            h = gt * jax.nn.sigmoid(gt) * ut
            dst[s, lanes] = h.T.astype(BF)
            return 0

        lax.fori_loop(first, last, tile, 0)

    own = at(kb(0, 0) * 2 + q, HT)
    local["g"].wait()
    local["u"].wait()
    hidden(RA // 128, FH // 128, q, ht, own)
    pl.semaphore_wait(bar, 7)

    go("D2", "D3", "D4", "HB1a", "HB2a")
    hidden(0, FH // 128, o, hs, pl.ds(0, HT))
    go("HS")
    hidden(0, RA // 128, q, ht, own)
    go("D1", "W", "G", "U")
    got("HS")
    go("HYA", "HB1b", "HB2b", "HA1", "HA2", "HYB")

    order = ((0, 0), (3, 0), (1, 0), (0, 1), (3, 1), (1, 1), (2, 0), (2, 1))

    def serve1(s):
        if s == 0:
            got("HB1a", "HB2a", "HB1b", "HB2b")
            go("HB3", "HB4", "HYB2", "HYB3")
            got("D3", "D4", "D2")
            go("D6", "D7", "D5a", "D5b", "C30", "C10", "C01")
            local["dy"].wait()
            local["w"].wait()
            got("W", "D1")
        elif s == 1:
            got("C30")
        elif s == 2:
            got("C10")
        elif s == 3:
            got("HA1", "HA2")
            go("HA5a", "HA5b")
            got("HYA")
            go("HA3a", "HA4b", "HA3b", "HA4a")
            got("C01")
        elif s == 4:
            got("HB3", "HB4")
            go("HYB4", "HYB5")
            got("D6", "D7")
            go("D8a", "D8b", "C31", "C11")
            got("C31")
        elif s == 5:
            got("C11")
        elif s == 6:
            got("D5a", "D5b")
            go("C20")
            got("C20")
        elif s == 7:
            got("HA3a", "HA4b")
            go("HA6a", "HA6b")
            got("D8a", "D8b")
            go("C21")
            got("C21")

    def step1(s, _):
        for i in range(8):
            pl.when(s == i)(functools.partial(serve1, i))
        dz = fl = jnp.int32(0)
        for i, (a, b) in enumerate(order):
            dz = jnp.where(s == i, a, dz)
            fl = jnp.where(s == i, b, fl)
        c = cb(dz, fl)

        def tile(m, _):
            rows = at(m, MT)
            acc = None
            for p in range(2):
                d = lax.dot_general(wv[p, rows, :], dyv[p, at(c, TB), :], NT, preferred_element_type=F32)
                acc = d if acc is None else acc + d
            part[c, rows, :] = acc.astype(BF)
            return 0

        lax.fori_loop(0, FH // MT, tile, 0)
        return 0

    lax.fori_loop(0, 8, step1, 0)

    go("S1P", "S1M", "S2PS0", "S2MS0", "SYB2", "SYB1", "SYB3")

    def add(k, start, size, *others):
        def chunk(i, _):
            here = pl.ds(pl.multiple_of(start + i * 64, 64), 64)
            t = part[k, here, :].astype(F32)
            for ref, off in others:
                t = t + ref[pl.ds(pl.multiple_of(off + i * 64, 64), 64), :].astype(F32)
            part[k, here, :] = t.astype(BF)
            return 0

        lax.fori_loop(0, size // 64, chunk, 0)

    def serve2(s):
        if s == 0:
            got("HYB", "HYB2", "HYB3", "HYB4", "HYB5", "HA3b", "HA4a", "HA5a", "HA5b", "HA6a", "HA6b")
        elif s == 6:
            got("S1P", "S1M")
            add(kb(0, 1), 0, HA, (r1p, 0))
            add(kb(1, 3), 0, HA, (r1m, 0))
            go("S2PC0", "S2MC0", "S2PS1", "S2MS1")
            add(kb(0, 1), HA, HA, (r1p, HA))
            add(kb(1, 3), HA, HA, (r1m, HA))
            go("S2PC1", "S2MC1")
            got("SYB2")
            add(kb(0, 2), RA, RB, (by.at[(x + 2) % 4], 0))
            go("SB1P", "SB1M")
        elif s == 13:
            got("S2PS0", "S2MC0")
            add(kb(1, 0), 0, HA, (r2ps, 0), (r2mc, 0))
            go("SYA0", "SYB0", "GD0", "GD1")
            got("SYB1", "SYB3")
            add(kb(0, 1), RA, RB, (by.at[(x + 1) % 4], 0))
            add(kb(0, 3), RA, RB, (by.at[(x + 3) % 4], 0))
            go("SB2Pi", "SB2Mi")

    def step2(s, _):
        for i in (0, 6, 13):
            pl.when(s == i)(functools.partial(serve2, i))
        m = (s // 4) % 2
        rows, cols = at(m, MT), at(s % 4, NTILE)

        def tile(p):
            return lax.dot_general(ht[rows, :], dyv[p, :, cols], NN, preferred_element_type=F32).astype(BF)

        t = tile(jnp.where(s < 8, o, q))

        @pl.when(s < 8)
        def _():
            gdv[rows, cols] = t

        @pl.when(s >= 8)
        def _():
            gd_ref[pl.ds(pl.multiple_of(q * FH + m * MT, MT), MT), cols] = t

        return 0

    lax.fori_loop(0, 16, step2, 0)

    got("S2PS1", "S2MC1")
    add(kb(1, 0), HA, HA, (r2ps, HA), (r2mc, HA))
    go("SYA1")

    got("G", "U")

    def final(first, last, base, *others):
        def tile(i, _):
            s = at(i, 128)
            f = pl.ds(pl.multiple_of(q * FH + i * 128, 128), 128)
            for who, gr, ur, fi, dg, du, fo in ((q, gv, uv, f, gg_ref, gu_ref, f), (o, gp, upv, s, og, ou, s)):
                lanes = at(who, HT)
                t = part[kb(0, 0), s, lanes].astype(F32)
                for ref in others:
                    t = t + ref[at(i - base, 128), lanes].astype(F32)
                gh = t.T
                gt, ut = gr[:, fi].astype(F32), ur[:, fi].astype(F32)
                sig = jax.nn.sigmoid(gt)
                dg[:, fo] = (gh * ut * sig * (1.0 + gt * (1.0 - sig))).astype(BF)
                du[:, fo] = (gh * (gt * sig)).astype(BF)
            return 0

        lax.fori_loop(first, last, tile, 0)

    got("S2PC0", "S2MS0", "SYA0")
    final(0, HA // 128, 0, r2pc, r2ms, ry)
    go("OG0", "OU0")
    got("SB1P", "SB1M")
    add(kb(0, 1), RA, HB, (b1p, 0))
    add(kb(0, 3), RA + HB, HB, (b1m, 0))
    go("SB2Pd", "SB2Md")
    got("S2PC1", "S2MS1", "SYA1")
    final(HA // 128, RA // 128, 0, r2pc, r2ms, ry)
    go("OG1", "OU1")
    got("SYB0", "SB2Pi", "SB2Mi", "SB2Pd", "SB2Md")
    final(RA // 128, FH // 128, RA // 128, by.at[x], b2p, b2m)
    go("OG2", "OU2")

    got("GD0", "GD1", "OG0", "OU0", "OG1", "OU1", "OG2", "OU2")
    for n in D:
        D[n].wait_send()


def write_out(gg, gu, gd, gg_ref, gu_ref, gd_ref, sems):
    cs = [pltpu.make_async_copy(gg, gg_ref, sems.at[0]), pltpu.make_async_copy(gu, gu_ref, sems.at[1])]
    for i in range(2):
        rows = pl.ds(i * FH, FH)
        cs.append(pltpu.make_async_copy(gd.at[rows, :], gd_ref.at[rows, :], sems.at[2 + i]))
    for c in cs:
        c.start()
    for c in cs:
        c.wait()


def local(grad_out, gate_act, up_act, down_weight):
    hbm = pl.BlockSpec(memory_space=pltpu.HBM)
    vmem = pl.BlockSpec(memory_space=pltpu.VMEM)
    block = lambda *s: pltpu.VMEM(s, BF)
    shapes = (gate_act.shape, up_act.shape, down_weight.shape)
    held = pl.pallas_call(
        kernel,
        out_shape=tuple(block(*s) for s in shapes),
        in_specs=[hbm] * 4,
        out_specs=(vmem,) * 3,
        scratch_shapes=[
            block(2, FH, DB), block(2, 8 * TB, DB), block(FH, 8 * TB), block(FH, HT),
            block(HT, 2 * FH), block(HT, 2 * FH), block(HT, FH), block(HT, FH),
            block(8, FH, TB),
            block(RA, TB), block(RA, TB), block(RA, TB), block(RA, TB), block(RA, TB), block(RA, TB), block(RA, TB),
            block(4, RB, TB), block(HB, TB), block(HB, TB), block(RB, TB), block(RB, TB),
            block(FH, DB), block(HT, FH), block(HT, FH),
            pltpu.SemaphoreType.DMA((80,)), pltpu.SemaphoreType.DMA((80,)), pltpu.SemaphoreType.DMA((4,)),
        ],
        compiler_params=pltpu.CompilerParams(
            collective_id=0, has_side_effects=True, vmem_limit_bytes=52 * 2**20
        ),
        name="swiglu_down_backward",
    )(grad_out, gate_act, up_act, down_weight)
    return pl.pallas_call(
        write_out,
        out_shape=tuple(jax.ShapeDtypeStruct(s, BF) for s in shapes),
        in_specs=[vmem] * 3,
        out_specs=(hbm,) * 3,
        scratch_shapes=[pltpu.SemaphoreType.DMA((4,))],
        compiler_params=pltpu.CompilerParams(vmem_limit_bytes=10 * 2**20),
        name="write_out",
    )(*held)


def solution(mesh):
    return jax.shard_map(
        local,
        mesh=mesh,
        in_specs=(P("col", "row"), P("row", "col"), P("row", "col"), P("col", "row")),
        out_specs=(P("row", "col"), P("row", "col"), P("col", "row")),
        check_vma=False,
    )
```

time: 125 us -> 107 us (0.86)
  local copies, waits for them, and re-layouts: 10.8 us -> 0 us
  Pallas kernels: 113 us -> 107 us
    unnamed x3 -> x0, local copies, waits for them, and re-layouts: 10.8 us -> none
    pallas_call x1 -> x2, Pallas kernels: 113 us -> 107 us  [the longest x1 103 us: local(): pl.pallas_call(kernel, out_shape=tuple((block(*s) for s in shapes)), in_s...]
where the time goes in v2:
time: 107 us
  Pallas kernels  107 us (100%)
    pallas_call x1, Pallas kernels, local(): pl.pallas_call(kernel, out_shape=tuple((block(*s) for s in shapes)), in_s...  103 us
    pallas_call x1, Pallas kernels, local(): pl.pallas_call(write_out, out_shape=tuple((jax.ShapeDtypeStruct(s, BF) fo...  3.47 us

profile of v2, /device:TPU:1, one launch (start us, length us, event | category | flops | bytes accessed | tf_op | source)
XLA Modules:
  0.0 107.3 jit_solution(6000330060932843537)
XLA Ops:
  0.6 103.2 %swiglu_down_backward.1 = (bf16[128,3328]{1,0:T(8,128)(2,1)S(1)}, bf16[128,3328]{1,0:T(8,128)(2,1)S(1)}, bf16[3328,1024]{1,0:T(8,128)(2,1)S(1)}) custom-call(bf16[256,1024]{1,0:T(8,128)(2,1)} %dy_ref.1, bf16[128,3328]{1,0:T(8,128)(2,1)} %gate_ref.1, bf16[128,3328]{1,0:T(8,128)(2,1)} %up_ref.1, bf16[3328,1024]{1,0:T(8,128)(2,1)} %w_ref.1), custom_call_target="tpu_custom_call" | custom-call | tf_op jit(solution)/shard_map/swiglu_down_backward/pallas_call | solution.py:381
  103.9 3.5 %write_out.1 = (bf16[128,3328]{1,0:T(8,128)(2,1)}, bf16[128,3328]{1,0:T(8,128)(2,1)}, bf16[3328,1024]{1,0:T(8,128)(2,1)}) custom-call(bf16[128,3328]{1,0:T(8,128)(2,1)S(1)} %get-tuple-element.6.gg, bf16[128,3328]{1,0:T(8,128)(2,1)S(1)} %get-tuple-element.7.gu, bf16[3328,1024]{1,0:T(8,128)(2,1)S(1)} %get-tuple-element.8.gd), custom_call_target="tpu_custom_call" | custom-call | tf_op jit(solution)/shard_map/write_out/pallas_call | solution.py:400

commit v3 on v2

--- a/solution.py
+++ b/solution.py
@@ -35,9 +35,8 @@
     return pl.ds(pl.multiple_of(i * size, size), size)
 
 
-def kernel(dy_ref, gate_ref, up_ref, w_ref, gg_ref, gu_ref, gd_ref,
-           wv, dyv, ht, hs, gv, uv, gp, upv, part, r1p, r1m, r2pc, r2ps, r2mc, r2ms, ry, by, b1p, b1m, b2p, b2m,
-           gdv, og, ou, ss, rs, ls):
+def kernel(dy_ref, gate_ref, up_ref, w_ref, gd_ref, tot, ry, b2p, b2m, fg, fu,
+           wv, dyv, ht, hs, gv, uv, part, r1p, r1m, r2pc, r2ps, r2mc, r2ms, by, b1p, b1m, gdv, tots, ss, rs, ls):
     row, col = lax.axis_index("row"), lax.axis_index("col")
     yl, x, q = row // 8, (row // 2) % 4, row % 2
     z, yh = col // 2, col % 2
@@ -53,6 +52,9 @@
     zp = dev(yl, x, q, (z + 1) % 4, yh)
     zm = dev(yl, x, q, (z + 3) % 4, yh)
     yhp = dev(yl, x, q, z, 1 - yh)
+    xpo = dev(yl, (x + 1) % 4, o, z, yh)
+    xmo = dev(yl, (x + 3) % 4, o, z, yh)
+    ylo = dev(1 - yl, x, o, z, yh)
 
     ids = {}
 
@@ -81,6 +83,9 @@
     def pt(fl, dx, rows):
         return part.at[kb(fl, dx), rows, :]
 
+    def ptc(fl, dx, rows, core_of):
+        return part.at[kb(fl, dx), rows, at(core_of, HT)]
+
     def same(name, ref, to):
         return remote(name, ref, ref, to)
 
@@ -88,8 +93,6 @@
 
     D = {
         "HS": remote("HS", hs, hth(pl.ds(0, FH), q), core),
-        "G": remote("G", gate_ref.at[:, half_o], gp, core),
-        "U": remote("U", up_ref.at[:, half_o], upv, core),
         "D1": remote("D1", dy_ref, dyb(q, 0, 0), core),
         "D2": remote("D2", dy_ref, dyb(q, 0, 0), yhp),
         "D3": remote("D3", dy_ref, dyb(q, 0, 0), zp),
@@ -127,17 +130,14 @@
         "S1M": remote("S1M", pt(1, 2, A), r1m, xm),
         "SB1P": remote("SB1P", pt(0, 2, B0), b1p, xp),
         "SB1M": remote("SB1M", pt(0, 2, B1), b1m, xm),
-        "SB2Pi": remote("SB2Pi", pt(0, 1, B1), b2p.at[pl.ds(HB, HB), :], xp),
-        "SB2Pd": remote("SB2Pd", pt(0, 1, B0), b2p.at[pl.ds(0, HB), :], xp),
-        "SB2Mi": remote("SB2Mi", pt(0, 3, B0), b2m.at[pl.ds(0, HB), :], xm),
-        "SB2Md": remote("SB2Md", pt(0, 3, B1), b2m.at[pl.ds(HB, HB), :], xm),
     }
     for i, r in enumerate((A0, A1)):
         D[f"S2PS{i}"] = remote(f"S2PS{i}", pt(1, 1, r), r2ps.at[r, :], xp)
         D[f"S2MS{i}"] = remote(f"S2MS{i}", pt(0, 3, r), r2ms.at[r, :], xm)
         D[f"S2PC{i}"] = remote(f"S2PC{i}", pt(0, 1, r), r2pc.at[r, :], xp)
         D[f"S2MC{i}"] = remote(f"S2MC{i}", pt(1, 3, r), r2mc.at[r, :], xm)
-        D[f"SYA{i}"] = remote(f"SYA{i}", pt(1, 0, r), ry.at[r, :], ylp)
+        for who, to, c in (("s", ylp, q), ("x", ylo, o)):
+            D[f"SYA{i}{who}"] = remote(f"SYA{i}{who}", ptc(1, 0, r, c), ry.at[q, r, :], to)
     for dx in range(4):
         D[f"SYB{dx}"] = remote(f"SYB{dx}", pt(1, dx, B), by.at[(x + dx) % 4], ylp)
     for dz, fl in ((3, 0), (1, 0), (0, 1), (2, 0), (1, 1), (3, 1), (2, 1)):
@@ -145,11 +145,12 @@
     for m in range(2):
         D[f"GD{m}"] = remote(f"GD{m}", gdv.at[pl.ds(m * MT, MT), :],
                              gd_ref.at[pl.ds(pl.multiple_of(q * FH + m * MT, MT), MT), :], core)
-    for name, start, size in (("0", 0, HA), ("1", HA, HA), ("2", RA, RB)):
-        there = pl.ds(pl.multiple_of(q * FH + start, 128), size)
-        here = pl.ds(start, size)
-        D["OG" + name] = remote("OG" + name, og.at[:, here], gg_ref.at[:, there], core)
-        D["OU" + name] = remote("OU" + name, ou.at[:, here], gu_ref.at[:, there], core)
+    for who, up_to, down_to, c in (("s", xp, xm, q), ("x", xpo, xmo, o)):
+        for n, dx, rows, dst, first, to in (("SB2Pi", 1, B1, b2p, HB, up_to), ("SB2Pd", 1, B0, b2p, 0, up_to),
+                                            ("SB2Mi", 3, B0, b2m, 0, down_to), ("SB2Md", 3, B1, b2m, HB, down_to)):
+            D[n + who] = remote(n + who, ptc(0, dx, rows, c), dst.at[q, pl.ds(first, HB), :], to)
+    for n, rows in (("TA", A), ("TB", B)):
+        D[n] = remote(n, tots.at[rows, :], tot.at[q, rows, :], core)
 
     def go(*names):
         for n in names:
@@ -167,7 +168,7 @@
     }
 
     bar = pltpu.get_barrier_semaphore()
-    for to in (core, xp, xm, ylp, zp, zm, yhp):
+    for to in (core, xp, xm, ylp, zp, zm, yhp, xpo, xmo, ylo):
         pl.semaphore_signal(bar, inc=1, device_id=to, device_id_type=MESH)
     for n in ("g", "u", "dy", "w"):
         local[n].start()
@@ -187,15 +188,23 @@
     local["g"].wait()
     local["u"].wait()
     hidden(RA // 128, FH // 128, q, ht, own)
-    pl.semaphore_wait(bar, 7)
+    pl.semaphore_wait(bar, 10)
 
     go("D2", "D3", "D4", "HB1a", "HB2a")
     hidden(0, FH // 128, o, hs, pl.ds(0, HT))
     go("HS")
     hidden(0, RA // 128, q, ht, own)
-    go("D1", "W", "G", "U")
+    go("D1", "W")
     got("HS")
     go("HYA", "HB1b", "HB2b", "HA1", "HA2", "HYB")
+
+    def factors(i, _):
+        f = at(i, 128)
+        gt, ut = gv[:, f].astype(F32), uv[:, f].astype(F32)
+        sig = jax.nn.sigmoid(gt)
+        fg[:, f] = ut * sig * (1.0 + gt * (1.0 - sig))
+        fu[:, f] = gt * sig
+        return 0
 
     order = ((0, 0), (3, 0), (1, 0), (0, 1), (3, 1), (1, 1), (2, 0), (2, 1))
 
@@ -211,6 +220,7 @@
         elif s == 1:
             got("C30")
         elif s == 2:
+            lax.fori_loop(0, 2 * FH // 128, factors, 0)
             got("C10")
         elif s == 3:
             got("HA1", "HA2")
@@ -290,11 +300,11 @@
         elif s == 13:
             got("S2PS0", "S2MC0")
             add(kb(1, 0), 0, HA, (r2ps, 0), (r2mc, 0))
-            go("SYA0", "SYB0", "GD0", "GD1")
+            go("SYA0s", "SYA0x", "SYB0", "GD0", "GD1")
             got("SYB1", "SYB3")
             add(kb(0, 1), RA, RB, (by.at[(x + 1) % 4], 0))
             add(kb(0, 3), RA, RB, (by.at[(x + 3) % 4], 0))
-            go("SB2Pi", "SB2Mi")
+            go("SB2Pis", "SB2Mis", "SB2Pix", "SB2Mix")
 
     def step2(s, _):
         for i in (0, 6, 13):
@@ -321,54 +331,72 @@
 
     got("S2PS1", "S2MC1")
     add(kb(1, 0), HA, HA, (r2ps, HA), (r2mc, HA))
-    go("SYA1")
-
-    got("G", "U")
-
-    def final(first, last, base, *others):
-        def tile(i, _):
-            s = at(i, 128)
-            f = pl.ds(pl.multiple_of(q * FH + i * 128, 128), 128)
-            for who, gr, ur, fi, dg, du, fo in ((q, gv, uv, f, gg_ref, gu_ref, f), (o, gp, upv, s, og, ou, s)):
-                lanes = at(who, HT)
-                t = part[kb(0, 0), s, lanes].astype(F32)
-                for ref in others:
-                    t = t + ref[at(i - base, 128), lanes].astype(F32)
-                gh = t.T
-                gt, ut = gr[:, fi].astype(F32), ur[:, fi].astype(F32)
-                sig = jax.nn.sigmoid(gt)
-                dg[:, fo] = (gh * ut * sig * (1.0 + gt * (1.0 - sig))).astype(BF)
-                du[:, fo] = (gh * (gt * sig)).astype(BF)
-            return 0
-
-        lax.fori_loop(first, last, tile, 0)
-
-    got("S2PC0", "S2MS0", "SYA0")
-    final(0, HA // 128, 0, r2pc, r2ms, ry)
-    go("OG0", "OU0")
+    go("SYA1s", "SYA1x")
     got("SB1P", "SB1M")
     add(kb(0, 1), RA, HB, (b1p, 0))
     add(kb(0, 3), RA + HB, HB, (b1m, 0))
-    go("SB2Pd", "SB2Md")
-    got("S2PC1", "S2MS1", "SYA1")
-    final(HA // 128, RA // 128, 0, r2pc, r2ms, ry)
-    go("OG1", "OU1")
-    got("SYB0", "SB2Pi", "SB2Mi", "SB2Pd", "SB2Md")
-    final(RA // 128, FH // 128, RA // 128, by.at[x], b2p, b2m)
-    go("OG2", "OU2")
-
-    got("GD0", "GD1", "OG0", "OU0", "OG1", "OU1", "OG2", "OU2")
+    go("SB2Pds", "SB2Mds", "SB2Pdx", "SB2Mdx")
+
+    def total(start, size, *others):
+        def chunk(i, _):
+            here = pl.ds(pl.multiple_of(start + i * 64, 64), 64)
+            off = at(i, 64)
+            for c, dst in ((q, tot.at[q]), (o, tots)):
+                lanes = at(c, HT)
+                t = part[kb(0, 0), here, lanes].astype(F32)
+                for ref in others:
+                    t = t + ref[off, lanes].astype(F32)
+                dst[here, :] = t
+            return 0
+
+        lax.fori_loop(0, size // 64, chunk, 0)
+
+    got("S2PC0", "S2MS0", "S2PC1", "S2MS1")
+    total(0, RA, r2pc, r2ms)
+    go("TA")
+    got("SYB0")
+    total(RA, RB, by.at[x])
+    go("TB")
+
+    got("GD0", "GD1", "TA", "TB", "SYA0s", "SYA0x", "SYA1s", "SYA1x")
+    for n in D:
+        if n.startswith("SB2"):
+            D[n].wait_recv()
     for n in D:
         D[n].wait_send()
 
 
-def write_out(gg, gu, gd, gg_ref, gu_ref, gd_ref, sems):
-    cs = [pltpu.make_async_copy(gg, gg_ref, sems.at[0]), pltpu.make_async_copy(gu, gu_ref, sems.at[1])]
-    for i in range(2):
-        rows = pl.ds(i * FH, FH)
-        cs.append(pltpu.make_async_copy(gd.at[rows, :], gd_ref.at[rows, :], sems.at[2 + i]))
-    for c in cs:
+def finish(gd, tot, ry, b2p, b2m, fg, fu, gg_ref, gu_ref, gd_ref, og, ou, sems):
+    cs = []
+
+    def put(src, dst):
+        c = pltpu.make_async_copy(src, dst, sems.at[len(cs)])
         c.start()
+        cs.append(c)
+
+    for h in range(2):
+        rows = pl.ds(h * FH, FH)
+        put(gd.at[rows, :], gd_ref.at[rows, :])
+    for h in range(2):
+        def tile(first, *others):
+            def body(i, _):
+                s = at(i, 128)
+                f = pl.ds(pl.multiple_of(h * FH + i * 128, 128), 128)
+                t = tot[h, s, :]
+                for ref in others:
+                    t = t + ref[h, at(i - first, 128), :].astype(F32)
+                gh = t.T
+                og[:, f] = (gh * fg[:, f]).astype(BF)
+                ou[:, f] = (gh * fu[:, f]).astype(BF)
+                return 0
+
+            return body
+
+        lax.fori_loop(0, RA // 128, tile(0, ry), 0)
+        lax.fori_loop(RA // 128, FH // 128, tile(RA // 128, b2p, b2m), 0)
+        cols = pl.ds(h * FH, FH)
+        put(og.at[:, cols], gg_ref.at[:, cols])
+        put(ou.at[:, cols], gu_ref.at[:, cols])
     for c in cs:
         c.wait()
 
@@ -377,34 +405,38 @@
     hbm = pl.BlockSpec(memory_space=pltpu.HBM)
     vmem = pl.BlockSpec(memory_space=pltpu.VMEM)
     block = lambda *s: pltpu.VMEM(s, BF)
-    shapes = (gate_act.shape, up_act.shape, down_weight.shape)
+    wide = lambda *s: pltpu.VMEM(s, F32)
+    tokens, weight = gate_act.shape, down_weight.shape
     held = pl.pallas_call(
         kernel,
-        out_shape=tuple(block(*s) for s in shapes),
+        out_shape=(
+            block(*weight), wide(2, FH, HT), block(2, RA, HT), block(2, RB, HT), block(2, RB, HT),
+            wide(*tokens), wide(*tokens),
+        ),
         in_specs=[hbm] * 4,
-        out_specs=(vmem,) * 3,
+        out_specs=(vmem,) * 7,
         scratch_shapes=[
             block(2, FH, DB), block(2, 8 * TB, DB), block(FH, 8 * TB), block(FH, HT),
-            block(HT, 2 * FH), block(HT, 2 * FH), block(HT, FH), block(HT, FH),
+            block(HT, 2 * FH), block(HT, 2 * FH),
             block(8, FH, TB),
-            block(RA, TB), block(RA, TB), block(RA, TB), block(RA, TB), block(RA, TB), block(RA, TB), block(RA, TB),
-            block(4, RB, TB), block(HB, TB), block(HB, TB), block(RB, TB), block(RB, TB),
-            block(FH, DB), block(HT, FH), block(HT, FH),
-            pltpu.SemaphoreType.DMA((80,)), pltpu.SemaphoreType.DMA((80,)), pltpu.SemaphoreType.DMA((4,)),
+            block(RA, TB), block(RA, TB), block(RA, TB), block(RA, TB), block(RA, TB), block(RA, TB),
+            block(4, RB, TB), block(HB, TB), block(HB, TB),
+            block(FH, DB), wide(FH, HT),
+            pltpu.SemaphoreType.DMA((90,)), pltpu.SemaphoreType.DMA((90,)), pltpu.SemaphoreType.DMA((4,)),
         ],
         compiler_params=pltpu.CompilerParams(
-            collective_id=0, has_side_effects=True, vmem_limit_bytes=52 * 2**20
+            collective_id=0, has_side_effects=True, vmem_limit_bytes=46 * 2**20
         ),
         name="swiglu_down_backward",
     )(grad_out, gate_act, up_act, down_weight)
     return pl.pallas_call(
-        write_out,
-        out_shape=tuple(jax.ShapeDtypeStruct(s, BF) for s in shapes),
-        in_specs=[vmem] * 3,
+        finish,
+        out_shape=tuple(jax.ShapeDtypeStruct(s, BF) for s in (tokens, tokens, weight)),
+        in_specs=[vmem] * 7,
         out_specs=(hbm,) * 3,
-        scratch_shapes=[pltpu.SemaphoreType.DMA((4,))],
-        compiler_params=pltpu.CompilerParams(vmem_limit_bytes=10 * 2**20),
-        name="write_out",
+        scratch_shapes=[block(*tokens), block(*tokens), pltpu.SemaphoreType.DMA((6,))],
+        compiler_params=pltpu.CompilerParams(vmem_limit_bytes=6 * 2**20),
+        name="finish",
     )(*held)
 
 

time: 107 us -> 106 us (level)
  Pallas kernels: 107 us -> 105 us
    pallas_call x2, Pallas kernels: 107 us -> 105 us  [the longest x1 101 us: local(): pl.pallas_call(kernel, out_shape=(block(*weight), wide(2, FH, HT), block(...]
where the time goes in v3:
time: 106 us; the launch traced here: 105 us
  Pallas kernels  105 us (99%)
    pallas_call x1, Pallas kernels, local(): pl.pallas_call(kernel, out_shape=(block(*weight), wide(2, FH, HT), block(...  101 us
    pallas_call x1, Pallas kernels, local(): pl.pallas_call(finish, out_shape=tuple((jax.ShapeDtypeStruct(s, BF) for s...  3.71 us

profile of v3, /device:TPU:1, one launch (start us, length us, event | category | flops | bytes accessed | tf_op | source)
XLA Modules:
  0.0 105.4 jit_solution(4728482191369976467)
XLA Ops:
  0.6 101.0 %swiglu_down_backward.1 = (bf16[3328,1024]{1,0:T(8,128)(2,1)S(1)}, f32[2,1664,128]{2,1,0:T(8,128)S(1)}, bf16[2,1024,128]{2,1,0:T(8,128)(2,1)S(1)}, bf16[2,640,12...) custom-call(bf16[256,1024]{1,0:T(8,128)(2,1)} %dy_ref.1, ...), custom_call_target="tpu_custom_call" | custom-call | tf_op jit(solution)/shard_map/swiglu_down_backward/pallas_call | solution.py:410
  101.7 3.7 %finish.1 = (bf16[128,3328]{1,0:T(8,128)(2,1)}, bf16[128,3328]{1,0:T(8,128)(2,1)}, bf16[3328,1024]{1,0:T(8,128)(2,1)}) custom-call(bf16[3328,1024]{1,0:T(8,128)(2,1)S(1)} %get-tuple-element.10.gd, f32[2,1664,128]{2,1,0:T(8,128)S(1)} %get-tuple-element.11.tot, bf16[2,1024,128]{2,1,0:T(8,128)(2,1)S(1)} %get-tuple-element.12.ry, ...), custom_call_target="tpu_custom_call" | custom-call | tf_op jit(solution)/shard_map/finish/pallas_call | solution.py:432

commit v4 on v3

--- a/solution.py
+++ b/solution.py
@@ -27,6 +27,16 @@
 B = pl.ds(RA, RB)
 B0 = pl.ds(RA, HB)
 B1 = pl.ds(RA + HB, HB)
+GA = 1056
+GB = FH - GA
+GHA = GA // 2
+GHB = GB // 2
+GA_ = pl.ds(0, GA)
+GA0 = pl.ds(0, GHA)
+GA1 = pl.ds(GHA, GHA)
+GB_ = pl.ds(GA, GB)
+GB0 = pl.ds(GA, GHB)
+GB1 = pl.ds(GA + GHB, GHB)
 MT = 832
 NTILE = 256
 
@@ -104,28 +114,28 @@
         "D7": same("D7", dyb(q, 0, 1), zm),
         "D8a": same("D8a", dyh(3, 1, 0), zp),
         "D8b": same("D8b", dyh(1, 1, 1), zm),
-        "HB1a": same("HB1a", hth(B, q), xp),
-        "HB1b": same("HB1b", hth(B, o), xp),
-        "HB2a": same("HB2a", hth(B, q), xm),
-        "HB2b": same("HB2b", hth(B, o), xm),
-        "HA1": same("HA1", htb(A, 0, 0), xp),
-        "HA2": same("HA2", htb(A, 0, 0), xm),
-        "HYA": same("HYA", htb(A, 0, 0), ylp),
-        "HYB": same("HYB", htb(B, 0, 0), ylp),
-        "HB3": same("HB3", htb(B0, 0, 3), xp),
-        "HB4": same("HB4", htb(B1, 0, 1), xm),
-        "HYB2": same("HYB2", htb(B, 0, 3), ylp),
-        "HYB3": same("HYB3", htb(B, 0, 1), ylp),
-        "HYB4": same("HYB4", htb(B0, 0, 2), ylp),
-        "HYB5": same("HYB5", htb(B1, 0, 2), ylp),
-        "HA3a": same("HA3a", htb(A0, 1, 0), xp),
-        "HA3b": same("HA3b", htb(A1, 1, 0), xp),
-        "HA4a": same("HA4a", htb(A0, 1, 0), xm),
-        "HA4b": same("HA4b", htb(A1, 1, 0), xm),
-        "HA5a": same("HA5a", htb(A0, 0, 3), xp),
-        "HA5b": same("HA5b", htb(A1, 0, 1), xm),
-        "HA6a": same("HA6a", htb(A0, 1, 3), xp),
-        "HA6b": same("HA6b", htb(A1, 1, 1), xm),
+        "HB1a": same("HB1a", hth(GB_, q), xp),
+        "HB1b": same("HB1b", hth(GB_, o), xp),
+        "HB2a": same("HB2a", hth(GB_, q), xm),
+        "HB2b": same("HB2b", hth(GB_, o), xm),
+        "HA1": same("HA1", htb(GA_, 0, 0), xp),
+        "HA2": same("HA2", htb(GA_, 0, 0), xm),
+        "HYA": same("HYA", htb(GA_, 0, 0), ylp),
+        "HYB": same("HYB", htb(GB_, 0, 0), ylp),
+        "HB3": same("HB3", htb(GB0, 0, 3), xp),
+        "HB4": same("HB4", htb(GB1, 0, 1), xm),
+        "HYB2": same("HYB2", htb(GB_, 0, 3), ylp),
+        "HYB3": same("HYB3", htb(GB_, 0, 1), ylp),
+        "HYB4": same("HYB4", htb(GB0, 0, 2), ylp),
+        "HYB5": same("HYB5", htb(GB1, 0, 2), ylp),
+        "HA3a": same("HA3a", htb(GA0, 1, 0), xp),
+        "HA3b": same("HA3b", htb(GA1, 1, 0), xp),
+        "HA4a": same("HA4a", htb(GA0, 1, 0), xm),
+        "HA4b": same("HA4b", htb(GA1, 1, 0), xm),
+        "HA5a": same("HA5a", htb(GA0, 0, 3), xp),
+        "HA5b": same("HA5b", htb(GA1, 0, 1), xm),
+        "HA6a": same("HA6a", htb(GA0, 1, 3), xp),
+        "HA6b": same("HA6b", htb(GA1, 1, 1), xm),
         "S1P": remote("S1P", pt(0, 2, A), r1p, xp),
         "S1M": remote("S1M", pt(1, 2, A), r1m, xm),
         "SB1P": remote("SB1P", pt(0, 2, B0), b1p, xp),
@@ -220,7 +230,6 @@
         elif s == 1:
             got("C30")
         elif s == 2:
-            lax.fori_loop(0, 2 * FH // 128, factors, 0)
             got("C10")
         elif s == 3:
             got("HA1", "HA2")
@@ -285,6 +294,7 @@
 
     def serve2(s):
         if s == 0:
+            lax.fori_loop(0, 2 * FH // 128, factors, 0)
             got("HYB", "HYB2", "HYB3", "HYB4", "HYB5", "HA3b", "HA4a", "HA5a", "HA5b", "HA6a", "HA6b")
         elif s == 6:
             got("S1P", "S1M")
@@ -374,8 +384,8 @@
         c.start()
         cs.append(c)
 
-    for h in range(2):
-        rows = pl.ds(h * FH, FH)
+    for i in range(8):
+        rows = pl.ds(i * (FH // 4), FH // 4)
         put(gd.at[rows, :], gd_ref.at[rows, :])
     for h in range(2):
         def tile(first, *others):
@@ -392,8 +402,8 @@
 
             return body
 
-        lax.fori_loop(0, RA // 128, tile(0, ry), 0)
-        lax.fori_loop(RA // 128, FH // 128, tile(RA // 128, b2p, b2m), 0)
+        lax.fori_loop(0, RA // 128, tile(0, ry), 0, unroll=True)
+        lax.fori_loop(RA // 128, FH // 128, tile(RA // 128, b2p, b2m), 0, unroll=True)
         cols = pl.ds(h * FH, FH)
         put(og.at[:, cols], gg_ref.at[:, cols])
         put(ou.at[:, cols], gu_ref.at[:, cols])
@@ -434,7 +444,7 @@
         out_shape=tuple(jax.ShapeDtypeStruct(s, BF) for s in (tokens, tokens, weight)),
         in_specs=[vmem] * 7,
         out_specs=(hbm,) * 3,
-        scratch_shapes=[block(*tokens), block(*tokens), pltpu.SemaphoreType.DMA((6,))],
+        scratch_shapes=[block(*tokens), block(*tokens), pltpu.SemaphoreType.DMA((12,))],
         compiler_params=pltpu.CompilerParams(vmem_limit_bytes=6 * 2**20),
         name="finish",
     )(*held)

time: 106 us -> 105 us (level)
  no operation moved by 1% of the time
where the time goes in v4:
time: 105 us
  Pallas kernels  105 us (100%)
    pallas_call x1, Pallas kernels, local(): pl.pallas_call(kernel, out_shape=(block(*weight), wide(2, FH, HT), block(...  101 us
    pallas_call x1, Pallas kernels, local(): pl.pallas_call(finish, out_shape=tuple((jax.ShapeDtypeStruct(s, BF) for s...  3.42 us

profile of v4, /device:TPU:1, one launch (start us, length us, event | category | flops | bytes accessed | tf_op | source)
XLA Modules:
  0.0 105.3 jit_solution(10914292698052155844)
XLA Ops:
  0.6 101.2 %swiglu_down_backward.1 = (bf16[3328,1024]{1,0:T(8,128)(2,1)S(1)}, f32[2,1664,128]{2,1,0:T(8,128)S(1)}, bf16[2,1024,128]{2,1,0:T(8,128)(2,1)S(1)}, bf16[2,640,12...) custom-call(bf16[256,1024]{1,0:T(8,128)(2,1)} %dy_ref.1, ...), custom_call_target="tpu_custom_call" | custom-call | tf_op jit(solution)/shard_map/swiglu_down_backward/pallas_call | solution.py:420
  101.9 3.4 %finish.1 = (bf16[128,3328]{1,0:T(8,128)(2,1)}, bf16[128,3328]{1,0:T(8,128)(2,1)}, bf16[3328,1024]{1,0:T(8,128)(2,1)}) custom-call(bf16[3328,1024]{1,0:T(8,128)(2,1)S(1)} %get-tuple-element.10.gd, f32[2,1664,128]{2,1,0:T(8,128)S(1)} %get-tuple-element.11.tot, bf16[2,1024,128]{2,1,0:T(8,128)(2,1)S(1)} %get-tuple-element.12.ry, ...), custom_call_target="tpu_custom_call" | custom-call | tf_op jit(solution)/shard_map/finish/pallas_call | solution.py:442
